TPU v7x, 1024 devices: a whole 8x8x8 slice. The times are simulated.
1024 devices in a mesh: ctx: 8 (over y), mp: 128 (over z, x, core).
Axes of the slice: x: 8, y: 8, z: 8, core: 2. Of those that a mesh axis runs over, the one named last changes fastest.
Arguments:
- tokens: bfloat16 [1536, 8192], P('ctx'), may hold values from -120 to 120
- norm_gain: float32 [8192], replicated, may hold values from 0.1 to 1.9
- in_weight: bfloat16 [8192, 3, 8192], P(None, None, 'mp'), may hold values from -0.0625 to 0.0625
- short_filter: float32 [3, 3, 8192], P(None, None, 'mp'), may hold values from -3 to 3
- rates: float32 [16, 8192], P(None, 'mp'), may hold values from 6.510417e-05 to 0.020833334
- residues: float32 [16, 8192], P(None, 'mp'), may hold values from -4 to 4
- skip: float32 [8192], P('mp'), may hold values from -4 to 4
- out_weight: bfloat16 [8192, 8192], P('mp'), may hold values from -0.25 to 0.25
- segment_ids: int32 [1536], replicated, may hold values from 0 to 7, never falling along the last dimension, each value on 1 to 576 neighbouring positions
Outputs:
- mixed: bfloat16 [1536, 8192], P('ctx', 'mp')
Inputs may be any that keep to these rules, and one draw needn't show every extreme that they name: `segment_ids`: never falls along the sequence; each document spans 1 to 576 positions.
All inputs are finite; a program needn't handle non-finite values.
Results may differ from a plain program's by a relative error of at most 0.0085.
Values may be sent and summed in bfloat16 or wider, within the bound.
A program may use at most 64 MiB of HBM per device.

v0:
```python
import jax
import jax.numpy as jnp
from jax import lax
from jax.sharding import Mesh
from jax.sharding import PartitionSpec as P

MP = ("mp_0", "mp_1", "mp_2")


epsilon = 1e-06


def shifted(value, axis, steps):
    count = lax.axis_size(axis)
    leading, last = (max(0, -steps), min(count, count - steps))
    return lax.ppermute(value, axis, [(source, source + steps) for source in range(leading, last)])


def copy_for_each(x, axis):
    copies = jnp.broadcast_to(x, (lax.axis_size(axis), *x.shape))
    return lax.all_to_all(copies, axis, split_axis=0, concat_axis=0, tiled=True)


def collected_together(x, axis):
    leaves = jax.tree.leaves(x)
    turns = sorted(range(len(leaves)), key=lambda k: -leaves[k].size)
    width = (1, *leaves[turns[0]].shape)[-1]
    lines = [
        jnp.pad(leaves[k].reshape(-1), (0, -leaves[k].size % width)).reshape(-1, width)
        for k in turns
    ]
    both, at, found = (copy_for_each(jnp.concatenate(lines), axis), 0, {})
    for k, line in zip(turns, lines):
        share = both[:, at : at + len(line)].reshape(len(both), -1)
        found[k] = share[:, : leaves[k].size].reshape(-1, *leaves[k].shape)
        at += len(line)
    numbers = iter(range(len(leaves)))
    return jax.tree.map(lambda _: found[next(numbers)], x)


def joined_by_halves(pieces, combine):
    while len(jax.tree.leaves(pieces)[0]) > 1:
        pieces = jax.vmap(combine)(
            *(jax.tree.map(lambda part: part[side::2], pieces) for side in (0, 1))
        )
    return jax.tree.map(lambda part: part[0], pieces)


def entering(x, axis, combine, identity):
    length, here = (lax.axis_size(axis), lax.axis_index(axis))
    passed = jnp.arange(length) < here

    def kept(part, zero, own):
        part = jnp.where(
            passed.reshape(-1, *(1 for _ in own.shape)), part, jnp.asarray(zero, own.dtype)
        )
        return part

    pieces = collected_together(x, axis)
    return joined_by_halves(jax.tree.map(kept, pieces, identity, x), combine)


def reduced_to_own(tiles, axes, turns):
    inside = tiles.shape[1:]
    tiles = tiles.reshape(*(lax.axis_size(a) for a in axes), *inside)
    tiles = jnp.moveaxis(tiles, turns, range(len(axes))).reshape(-1, *inside)
    for k in turns:
        tiles = lax.psum_scatter(tiles, axes[k], scatter_dimension=0, tiled=True)
    return tiles[0]


def in_blocks(x, dim, length):
    shape = x.shape
    tiles = x.reshape(*shape[:dim], length, shape[dim] // length, *shape[dim + 1 :])
    return jnp.moveaxis(tiles, dim, 0)


def sum_by_axis(x, axes, turns, dim):
    length = lax.axis_size(axes)
    return reduced_to_own(in_blocks(x, dim, length), axes, turns)


def project(block, norm_gain, weights):
    floats = block.astype(jnp.float32)
    mean_square = jnp.mean(floats * floats, axis=-1, keepdims=True)
    normed = (floats * lax.rsqrt(mean_square + epsilon) * norm_gain[None, :]).astype(jnp.bfloat16)
    return jnp.dot(normed, weights, preferred_element_type=jnp.float32).astype(jnp.bfloat16)


def local(
    tokens, norm_gain, in_weight, short_filter, rates, residues, skip, out_weight, segment_ids
):
    tok_rows = tokens.shape[0]
    model_width = tokens.shape[1]
    channels = in_weight.shape[2]
    filter_taps = short_filter.shape[0]
    pole_count = rates.shape[0]
    device_index = lax.axis_index("ctx")
    row_offset = device_index * tok_rows
    weights = in_weight.reshape(model_width, 3 * channels)
    projected = project(tokens, norm_gain, weights)
    previous = shifted(projected[tok_rows - (filter_taps - 1) :], "ctx", 1)
    extended = jnp.concatenate([previous, projected], axis=0)
    padded_ids = jnp.concatenate([jnp.full((filter_taps,), -1, jnp.int32), segment_ids], axis=0)
    window = lax.dynamic_slice_in_dim(padded_ids, row_offset, tok_rows + filter_taps, 0)
    local_ids = window[filter_taps:]
    taps_table = short_filter.reshape(filter_taps, 3 * channels)
    featured = jnp.zeros((tok_rows, 3 * channels), jnp.float32)
    for lag_index in range(filter_taps):
        begin = filter_taps - 1 - lag_index
        lagged = extended[begin : begin + tok_rows].astype(jnp.float32)
        matches = window[filter_taps - lag_index : filter_taps - lag_index + tok_rows] == local_ids
        term = taps_table[lag_index][None, :] * lagged
        featured = featured + jnp.where(matches[:, None], term, jnp.zeros_like(term))
    query_part = featured[:, :channels]
    key_part = featured[:, channels : 2 * channels]
    value_part = featured[:, 2 * channels :]
    product = key_part * value_part
    offsets = jnp.arange(tok_rows, dtype=jnp.float32)
    center = float(tok_rows // 2)
    growth = jnp.exp(-(offsets - center)[:, None, None] * rates[None])
    shrinkage = jnp.exp((offsets - center)[:, None, None] * rates[None])
    weighted = (shrinkage * product[:, None, :]).reshape(tok_rows, pole_count * channels)
    visible = (offsets[:, None] >= offsets[None, :]) & (local_ids[:, None] == local_ids[None, :])
    in_block = jnp.dot(visible.astype(jnp.float32), weighted, precision=lax.Precision.HIGHEST)
    in_block = in_block.reshape(tok_rows, pole_count, channels) * growth
    survives = local_ids == window[filter_taps - 1]
    block_factor = jnp.exp(-rates * tok_rows)
    block_end = in_block[tok_rows - 1]
    block_decay = block_factor * survives[tok_rows - 1].astype(jnp.float32)

    def combine(earlier, later):
        return (earlier[0] * later[0], earlier[1] * later[0] + later[1])

    identity = (jnp.ones_like(block_end), jnp.zeros_like(block_end))
    _, incoming = entering((block_decay, block_end), "ctx", combine, identity)
    carried = incoming[None] * jnp.exp(-(offsets + 1.0)[:, None, None] * rates[None])
    carried = carried * survives.astype(jnp.float32)[:, None, None]
    states = in_block + carried
    pole_weight = residues * jnp.sqrt(-jnp.expm1(-2.0 * rates))
    longconv = jnp.sum(pole_weight[None] * states, axis=1)
    gated = (query_part * (longconv + skip[None, :] * product)).astype(jnp.bfloat16)
    partial_terms = jnp.dot(gated, out_weight, preferred_element_type=jnp.float32)
    return sum_by_axis(partial_terms, MP, (2, 0, 1), 1).astype(jnp.bfloat16)


def solution(mesh):
    torus = Mesh(mesh.devices.reshape(mesh.shape["ctx"], 8, 8, 2), ("ctx", "mp_0", "mp_1", "mp_2"))
    placed = (
        P("ctx", None),
        P(),
        P(None, None, MP),
        P(None, None, MP),
        P(None, MP),
        P(None, MP),
        P(MP),
        P(MP, None),
        P(),
    )
    return jax.shard_map(
        local, mesh=torus, in_specs=placed, out_specs=P("ctx", MP), check_vma=False
    )
```

profile of v0, /device:TPU:2, one launch (start us, length us, event | category | flops | bytes accessed | tf_op | source)
XLA Modules:
  0.0 209.7 jit_solution(10359515062612510825)
XLA Ops:
  6.5 0.0 copy-start
  6.5 2.8 %fusion = f32[192]{0:T(256)S(1)} fusion(bf16[192,8192]{1,0:T(8,128)(2,1)} %param.9), kind=kLoop, calls=%fused_computation.2 | loop fusion | flops 4718400 | bytes 3146496 | tf_op jit(solution)/shard_map/reduce_sum | solution.py:85
  9.3 0.1 copy-done
  9.4 0.0 copy-start.4
  9.4 0.0 copy-start.6
  9.4 0.0 copy-start.2
  9.4 0.0 copy-start.5
  9.4 3.1 %fusion.7 = bf16[192,192]{0,1:T(8,128)(2,1)S(1)} fusion(bf16[8192,192]{0,1:T(8,128)(2,1)S(1)} %bitcast.26, bf16[192,8192]{1,0:T(8,128)(2,1)} %param.9, f32[8192]{0:T(1024)} %param.10, f32[192]{0:T(256)S(1)} %add_rsqrt_fusion), kind=kOutput, calls=%fused_computation.9 | convolution fusion | flops 610308096 | bytes 6398720 | tf_op jit(solution)/shard_map/dot_general | solution.py:87
  12.5 0.1 slice.119
  12.6 3.6 %collective-permute-start = (bf16[2,192]{0,1:T(8,128)(2,1)S(1)}, bf16[2,192]{0,1:T(8,128)(2,1)S(1)}, u32[]{:S(2)}, u32[]{:S(2)}) collective-permute-start(bf16[2,192]{0,1:T(8,128)(2,1)S(1)} %slice.119), channel_id=1, source_target_pairs={{0,128},{128,256},{256,384},{384,512},{512,640},{640,768},{768,896... | collective-permute-start | bytes 2312 | tf_op jit(solution)/shard_map/ppermute | solution.py:16
  16.2 0.6 fusion.22
  16.8 0.0 copy-done.4
  16.8 0.1 pad_dynamic-slice_fusion
  16.9 0.6 slice.103
  17.5 1.3 fusion.23
  18.8 0.6 slice.104
  20.0 0.0 copy-done.6
  20.0 0.0 copy-done.2
  20.0 0.0 copy-done.5
  20.0 0.6 sqrt_multiply_fusion
  20.7 0.6 iota_add_fusion
  21.2 0.7 slice.93
  21.9 0.7 mul.202
  22.6 0.6 mul.182
  23.2 0.7 mul.194
  23.8 0.6 mul.191
  24.5 0.0 copy-start.3
  24.5 0.0 collective-permute-done
  24.5 0.9 select_add_fusion
  25.4 0.9 bitcast_multiply_fusion
  26.3 1.5 convolution_multiply_fusion
  27.8 0.0 copy-start.1
  27.8 1.0 copy-done.1
  28.8 0.4 slice_reduce_fusion
  29.1 0.0 copy-done.3
  29.2 0.8 reshape.80
  29.9 6.7 %all-to-all-start = ((f32[8,1,2048]{2,1,0:T(1,128)}), f32[8,1,2048]{2,1,0:T(1,128)S(1)}, u32[]{:S(2)}, u32[]{:S(2)}) async-start(f32[8,1,2048]{2,1,0:T(1,128)} %reshape.80), calls=%async_computation | async-start | bytes 131072 | tf_op jit(solution)/shard_map/all_to_all | solution.py:21
  36.6 0.0 reduce-scatter.4.cloned.1.call-start
  36.6 0.5 iota_compare_fusion.1
  37.2 0.6 add_negate_fusion
  37.8 7.2 %all-to-all-done = f32[8,1,2048]{2,1,0:T(1,128)S(1)} async-done(((f32[8,1,2048]{2,1,0:T(1,128)}), f32[8,1,2048]{2,1,0:T(1,128)S(1)}, u32[]{:S(2)}, u32[]{:S(2)}) %all-to-all-start) | async-done | bytes 65568 | tf_op jit(solution)/shard_map/all_to_all | solution.py:21
  45.0 0.5 broadcast.62
  45.5 1.4 reduce.2
  46.9 0.9 reshape.81
  47.8 0.7 slice_select_fusion
  48.6 1.7 multiply_reduce_fusion
  50.3 2.6 %fusion.17 = f32[192,8192]{0,1:T(8,128)S(1)} fusion(bf16[64,8192]{1,0:T(8,128)(2,1)} %param.16, f32[192,192]{0,1:T(8,128)S(1)} %select_add_fusion, f32[192,64]{0,1:T(8,128)S(1)} %multiply_reduce_fusion, f32[192,64]{0,1:T(8,128)S(1)} %slice_multiply_fusion, f32[64]{0:T(128)} %param.15), kind=kOutput, calls=%fused_computation.26 | convolution fusion | flops 201375744 | bytes 7536896 | tf_op jit(solution)/shard_map/dot_general | solution.py:143
  52.9 3.8 %copy.12 = f32[2,8,8,192,64]{3,4,2,1,0:T(8,128)} copy(f32[2,8,8,192,64]{3,4,0,2,1:T(8,128)S(1)} %bitcast.28) | data formatting | bytes 12582912 | tf_op jit(solution)/shard_map/transpose | solution.py:66
  56.7 0.0 reduce-scatter.4.cloned.1.call-update
  56.7 0.0 reduce-scatter.6.cloned.1.call-start
  56.8 32.9 %reduce-scatter.4.cloned.1.call-done = f32[64,192,64]{1,2,0:T(8,128)} async-done(((f32[128,192,64]{1,2,0:T(8,128)}), f32[64,192,64]{1,2,0:T(8,128)}) %reduce-scatter.4.cloned.1.call-update) | async-done | bytes 3145744 | tf_op jit(solution)/shard_map/reduce_scatter | solution.py:68
  89.7 0.0 reduce-scatter.6.cloned.1.call-update
  89.8 0.0 reduce-scatter.8.cloned.1.call-start
  89.8 68.0 %reduce-scatter.6.cloned.1.call-done = f32[8,192,64]{1,2,0:T(8,128)} async-done(((f32[64,192,64]{1,2,0:T(8,128)}), f32[8,192,64]{1,2,0:T(8,128)}) %reduce-scatter.6.cloned.1.call-update) | async-done | bytes 393232 | tf_op jit(solution)/shard_map/reduce_scatter | solution.py:68
  157.8 0.0 reduce-scatter.8.cloned.1.call-update
  157.8 43.9 %reduce-scatter.8.cloned.1.call-done = f32[1,192,64]{1,2,0:T(8,128)} async-done(((f32[8,192,64]{1,2,0:T(8,128)}), f32[1,192,64]{1,2,0:T(8,128)}) %reduce-scatter.8.cloned.1.call-update) | async-done | bytes 49168 | tf_op jit(solution)/shard_map/reduce_scatter | solution.py:68
  201.7 1.5 convert_bitcast_fusion
  (8 shorter events, 0.1 us)
Async XLA Ops:
  6.5 2.8 %copy-start = (bf16[8192,3,64]{0,2,1:T(8,128)(2,1)S(1)}, bf16[8192,3,64]{0,2,1:T(8,128)(2,1)}, u32[]{:S(2)}) copy-start(bf16[8192,3,64]{0,2,1:T(8,128)(2,1)} %param.11) | copy-start | bytes 9437188
  9.4 7.4 %copy-start.4 = (s32[1536]{0:T(1024)S(1)}, s32[1536]{0:T(1024)}, u32[]{:S(2)}) copy-start(s32[1536]{0:T(1024)} %param.17) | copy-start | bytes 18436
  9.4 10.6 %copy-start.6 = (f32[3,3,64]{2,1,0:T(4,128)S(1)}, f32[3,3,64]{2,1,0:T(4,128)}, u32[]{:S(2)}) copy-start(f32[3,3,64]{2,1,0:T(4,128)} %param.12) | copy-start | bytes 6916
  9.4 10.6 %copy-start.2 = (f32[16,64]{1,0:T(8,128)S(1)}, f32[16,64]{1,0:T(8,128)}, u32[]{:S(2)}) copy-start(f32[16,64]{1,0:T(8,128)} %param.13) | copy-start | bytes 12292
  9.4 10.7 %copy-start.5 = (f32[16,64]{1,0:T(8,128)S(1)}, f32[16,64]{1,0:T(8,128)}, u32[]{:S(2)}) copy-start(f32[16,64]{1,0:T(8,128)} %param.14) | copy-start | bytes 12292
  12.6 11.9 %collective-permute-start = (bf16[2,192]{0,1:T(8,128)(2,1)S(1)}, bf16[2,192]{0,1:T(8,128)(2,1)S(1)}, u32[]{:S(2)}, u32[]{:S(2)}) collective-permute-start(bf16[2,192]{0,1:T(8,128)(2,1)S(1)} %slice.119), channel_id=1, source_target_pairs={{0,128},{128,256},{256,384},{384,512},{512,640},{640,768},{768,896... | collective-permute-start | bytes 2312 | tf_op jit(solution)/shard_map/ppermute | solution.py:16
  24.5 4.7 %copy-start.3 = (f32[16,64]{1,0:T(8,128)S(1)}, f32[16,64]{1,0:T(8,128)}, u32[]{:S(2)}) copy-start(f32[16,64]{1,0:T(8,128)} %get-tuple-element.15) | copy-start | bytes 12292
  27.8 1.0 copy-start.1
  29.9 15.0 %all-to-all-start = ((f32[8,1,2048]{2,1,0:T(1,128)}), f32[8,1,2048]{2,1,0:T(1,128)S(1)}, u32[]{:S(2)}, u32[]{:S(2)}) async-start(f32[8,1,2048]{2,1,0:T(1,128)} %reshape.80), calls=%async_computation | async-start | bytes 131072 | tf_op jit(solution)/shard_map/all_to_all | solution.py:21
  36.6 53.1 %reduce-scatter.4.cloned.1.call-start = ((), (), s32[]{:S(2)}) async-start(), calls=%async_computation.4 | async-start | bytes 12582912 | tf_op jit(solution)/shard_map/reduce_scatter | solution.py:68
  56.7 101.0 %reduce-scatter.6.cloned.1.call-start = ((), (), s32[]{:S(2)}) async-start(), calls=%async_computation.5 | async-start | bytes 4718592 | tf_op jit(solution)/shard_map/reduce_scatter | solution.py:68
  89.8 112.0 %reduce-scatter.8.cloned.1.call-start = ((), (), s32[]{:S(2)}) async-start(), calls=%async_computation.6 | async-start | bytes 589824 | tf_op jit(solution)/shard_map/reduce_scatter | solution.py:68
Sparse Core Ops, SparseCore 0:
  56.9 32.8 reduce-scatter.3
  93.1 64.5 reduce-scatter.5
  161.1 40.5 reduce-scatter.7
where the time goes:
time: 210 us
  waiting for transfers between devices  152 us (72%)
  other arithmetic  14.1 us (7%)
  between operations  13.9 us (7%)
  local copies, waits for them, and re-layouts  12.1 us (6%)
  starting transfers between devices  10.4 us (5%)
  matrix products  7.17 us (3%)
    reduce_scatter x3, waiting for transfers between devices, reduced_to_own(): tiles = lax.psum_scatter(tiles, axes[k], scatter_dimension=0, tiled=True)  145 us
    all_to_all x1, waiting for transfers between devices, copy_for_each(): return lax.all_to_all(copies, axis, split_axis=0, concat_axis=0, tiled=True)  7.22 us
    all_to_all x1, starting transfers between devices, copy_for_each(): return lax.all_to_all(copies, axis, split_axis=0, concat_axis=0, tiled=True)  6.66 us
  transfers between devices with their start and end apart: 5, of which 4 were waited for; matrix products, arithmetic and copies ran while one was open for 4% of the time, Pallas kernels for 0%

commit v1 on v0

v1 whole, which is shorter than its diff:
```python
import functools

import jax
import jax.numpy as jnp
from jax import lax
from jax.experimental import pallas as pl
from jax.experimental.pallas import tpu as pltpu
from jax.sharding import Mesh
from jax.sharding import PartitionSpec as P

MP = ("mp_0", "mp_1", "mp_2")
MESH = pl.DeviceIdType.MESH
F32 = jnp.float32
BF16 = jnp.bfloat16

epsilon = 1e-06

ROWS = 192
HALF = ROWS // 2
QUARTER = HALF // 2
CH = 64
POLES = 16
PAIRS = POLES // 2
WIDTH = 8192
DOCS = 8
CENTER = float(ROWS // 2)
CLASSES = 4
TOKEN_CHUNK = 2048
WEIGHT_CHUNK = 1024


def distances(count):
    return sorted(range(1, count), key=lambda d: -min(d, count - d))


def kernel(
    sizes,
    tokens, gain, in_weight, taps, rates, residues, skip, out_weight, ids,
    out,
    tok, win, wout, proj, halo, growth, weighted, visible, product, query, acc,
    lag_one, lag_two, survives, ends, incoming, a_send, a_recv, lhs, c_send, c_recv,
    tok_sem, win_sem, s1_send, s1_recv, s2_send, s2_recv, oc_send, oc_recv,
    halo_sem, e_send, e_recv, as_sem, ar_sem, cs_sem, cr_sem,
):
    ny, nz, nx = sizes
    y, z, x, c = (lax.axis_index(name) for name in ("ctx", *MP))
    other = 1 - c
    per_class = nz // CLASSES
    group = nx * CH

    def at_y(step):
        return (lax.rem(y + step + ny, ny), z, x, c)

    tok_loads = []
    for k in range(WIDTH // TOKEN_CHUNK):
        span = pl.ds(k * TOKEN_CHUNK, TOKEN_CHUNK)
        load = pltpu.make_async_copy(tokens.at[:, span], tok.at[:, span], tok_sem.at[k])
        load.start()
        tok_loads.append(load)
    win_loads = []
    for k in range(WIDTH // WEIGHT_CHUNK):
        span = pl.ds(k * WEIGHT_CHUNK, WEIGHT_CHUNK)
        for part, (source, target, count) in enumerate(((0, 0, 3 * CH), (2 * CH, 3 * CH, CH))):
            load = pltpu.make_async_copy(
                in_weight.at[pl.ds(source, count), span],
                win.at[pl.ds(target, count), span],
                win_sem.at[2 * k + part],
            )
            load.start()
            win_loads.append(load)

    barrier = pltpu.get_barrier_semaphore()
    greeted = [(y, z, x, other)]
    for parity in (c, other):
        greeted += [(y, z, lax.rem(x + d, nx), parity) for d in range(1, nx)]
        greeted += [(y, lax.rem(z + d, nz), x, parity) for d in range(1, nz)]
    steps = sorted({d % ny for d in (1, 2, 3, -1, -2, -3)})
    greeted += [at_y(d) for d in steps]
    for device in greeted:
        pl.semaphore_signal(barrier, inc=1, device_id=device, device_id_type=MESH)

    id_values = ids[...].astype(F32)
    bounds = [
        jnp.sum(jnp.where(id_values < float(k), 1.0, 0.0), axis=(0, 1), keepdims=True)
        for k in range(1, DOCS)
    ]

    def document(position):
        total = jnp.zeros_like(position)
        for bound in bounds:
            total = total + jnp.where(position >= bound, 1.0, 0.0)
        return total

    base = (y * ROWS).astype(F32)
    down = lax.broadcasted_iota(jnp.int32, (ROWS, 128), 0).astype(F32)
    own = document(down + base)

    def document_at(offset):
        return document(jnp.zeros((1, 128), F32) + (base + float(offset)))

    before = [document_at(-1 - ROWS * k) for k in range(3)]
    reach = [jnp.where(y >= k, 1.0, 0.0).astype(F32) for k in range(4)]
    survives[...] = jnp.where(own == before[0], reach[1], 0.0)
    lag_one[...] = jnp.where(own == document(down + (base - 1.0)), 1.0, 0.0)
    lag_two[...] = jnp.where(own == document(down + (base - 2.0)), 1.0, 0.0)
    whole = jnp.where(document_at(0) == document_at(ROWS - 1), 1.0, 0.0)
    across = lax.broadcasted_iota(jnp.int32, (1, 2 * ROWS), 1).astype(F32)
    across = jnp.where(across < float(ROWS), across, across - float(ROWS))
    beside = document(across + base)
    seen = (down[:, :1] >= across) & (own[:, :1] == beside)
    visible[...] = jnp.where(seen, 1.0, 0.0).astype(BF16)

    def paired(ref):
        return jnp.concatenate([ref[0:PAIRS, :], ref[PAIRS:POLES, :]], axis=1)

    rate = paired(rates)
    twice = -2.0 * rate
    small = twice * (1.0 + twice * (0.5 + twice * (1.0 / 6.0 + twice * (1.0 / 24.0 + twice * (
        1.0 / 120.0)))))
    weight = paired(residues) * jnp.sqrt(-small)

    squares = jnp.zeros((ROWS, 128), F32)
    for k in range(WIDTH // TOKEN_CHUNK):
        tok_loads[k].wait()
        for lane in range(k * TOKEN_CHUNK, (k + 1) * TOKEN_CHUNK, 128):
            piece = tok[:, lane : lane + 128].astype(F32)
            squares = squares + piece * piece
    mean_square = jnp.sum(squares, axis=1, keepdims=True) * (1.0 / WIDTH)
    scale = lax.rsqrt(mean_square + epsilon)

    pl.semaphore_wait(barrier, len(greeted))

    kind = lax.rem(y, CLASSES)

    def block(j, turned=0):
        return lax.rem(kind + turned + CLASSES, CLASSES) + CLASSES * j

    def columns(index):
        return pl.ds(pl.multiple_of(index * 128, 128), 128)

    mine = pl.ds(pl.multiple_of(c * group + x * CH, CH), CH)
    s1 = []
    for j in range(per_class):
        for i, d in enumerate(distances(nx)):
            there = lax.rem(x + d, nx)
            copy = pltpu.make_async_remote_copy(
                src_ref=out_weight.at[:, columns(block(j) * nx + there)],
                dst_ref=wout.at[mine, columns(block(j))],
                send_sem=s1_send.at[j * nx + i],
                recv_sem=s1_recv.at[j * nx + x],
                device_id=(y, z, there, c),
                device_id_type=MESH,
            )
            copy.start()
            s1.append(copy)
    kept = [
        pltpu.make_async_copy(
            out_weight.at[:, columns(block(j) * nx + x)],
            wout.at[mine, columns(block(j))],
            s1_recv.at[j * nx + x],
        )
        for j in range(per_class)
    ]
    for copy in kept:
        copy.start()

    acc[...] = jnp.zeros_like(acc)
    for k in range(WIDTH // WEIGHT_CHUNK):
        win_loads[2 * k].wait()
        win_loads[2 * k + 1].wait()
        span = pl.ds(k * WEIGHT_CHUNK, WEIGHT_CHUNK)
        normed = (tok[:, span].astype(F32) * scale * gain[:, span]).astype(BF16)
        acc[...] += lax.dot_general(
            normed, win[:, span], (((1,), (1,)), ((), ())), preferred_element_type=F32
        )
    proj[0:8, :] = jnp.zeros((8, 256), F32)
    proj[8 : 8 + ROWS, :] = acc[...].astype(BF16).astype(F32)
    halo_copy = pltpu.make_async_remote_copy(
        src_ref=proj.at[pl.ds(ROWS, 8)],
        dst_ref=halo,
        send_sem=halo_sem.at[0],
        recv_sem=halo_sem.at[1],
        device_id=at_y(1),
        device_id_type=MESH,
    )
    halo_copy.start()

    def is_low(count):
        return lax.broadcasted_iota(jnp.int32, (count, 128), 1) < CH

    tap_rows = []
    for j in range(3):
        first = jnp.concatenate([taps[j, 0:1, :], taps[j, 1:2, :]], axis=1)
        second = jnp.concatenate([taps[j, 2:3, :], taps[j, 2:3, :]], axis=1)
        tap_rows.append((first, second))

    def filtered(count):
        tiles = []
        for side in range(2):
            lanes = slice(128 * side, 128 * side + 128)
            total = tap_rows[0][side] * proj[8 : 8 + count, lanes]
            total = total + tap_rows[1][side] * (proj[7 : 7 + count, lanes] * lag_one[0:count, :])
            total = total + tap_rows[2][side] * (proj[6 : 6 + count, lanes] * lag_two[0:count, :])
            tiles.append(total)
        turned = pltpu.roll(tiles[0], CH, 1)
        side = is_low(count)
        return jnp.where(side, tiles[0], turned), jnp.where(side, turned, tiles[0]) * tiles[1]

    query_part, product_part = filtered(ROWS)
    query[...] = query_part
    product[...] = product_part

    offset = down - CENTER
    for g in range(PAIRS):
        lanes = slice(128 * g, 128 * g + 128)
        exponent = offset * rate[g : g + 1, :]
        value = jnp.exp(exponent) * product_part
        high = value.astype(BF16)
        weighted[0:ROWS, lanes] = high
        weighted[ROWS : 2 * ROWS, lanes] = (value - high.astype(F32)).astype(BF16)
        growth[:, lanes] = weight[g : g + 1, :] * jnp.exp(-exponent)
    last = []
    total = jnp.zeros((ROWS, 128), F32)
    for g in range(PAIRS):
        lanes = slice(128 * g, 128 * g + 128)
        inside = jnp.dot(visible[...], weighted[:, lanes], preferred_element_type=F32)
        last.append(inside[ROWS - 1 : ROWS, :])
        total = total + growth[:, lanes] * inside
    last = jnp.concatenate(last, axis=0)

    halo_copy.wait_recv()
    proj[0:8, :] = halo[...] * reach[1]
    query_top, product_top = filtered(8)
    change = product_top - product[0:8, :]
    query[0:8, :] = query_top
    product[0:8, :] = product_top
    change_zero = jnp.exp(-CENTER * rate) * change[0:1, :]
    change_one = jnp.exp((1.0 - CENTER) * rate) * change[1:2, :]
    ends[...] = jnp.exp((CENTER + 1.0 - ROWS) * rate) * (
        last + whole * (change_zero + change_one)
    )
    e_copies = []
    for k in range(3):
        copy = pltpu.make_async_remote_copy(
            src_ref=ends,
            dst_ref=incoming.at[k],
            send_sem=e_send.at[k],
            recv_sem=e_recv.at[k],
            device_id=at_y(k + 1),
            device_id_type=MESH,
        )
        copy.start()
        e_copies.append(copy)

    parity = pl.ds(pl.multiple_of(c * group, group), group)

    def passed_on(index, sem, target):
        return pltpu.make_async_remote_copy(
            src_ref=wout.at[parity, columns(index)],
            dst_ref=wout.at[parity, columns(index)],
            send_sem=s2_send.at[sem],
            recv_sem=s2_recv.at[sem],
            device_id=target,
            device_id_type=MESH,
        )

    def handed(index):
        return pltpu.make_async_remote_copy(
            src_ref=wout.at[parity, columns(index)],
            dst_ref=wout.at[parity, columns(index)],
            send_sem=oc_send.at[index],
            recv_sem=oc_recv.at[index],
            device_id=(y, z, x, other),
            device_id_type=MESH,
        )

    for j in range(per_class):
        for d in range(1, nx):
            there = lax.rem(x + d, nx)
            pltpu.make_async_copy(
                wout.at[mine, columns(block(j))],
                wout.at[mine, columns(block(j))],
                s1_recv.at[j * nx + there],
            ).wait()
        kept[j].wait()
    s2 = []
    handovers = []
    half_class = per_class // 2
    rightward = list(range(per_class))
    leftward = rightward[half_class:] + rightward[:half_class]
    for j, k in zip(rightward, leftward):
        for copy in (
            passed_on(block(j), j, at_y(1)),
            passed_on(block(k), per_class + k, at_y(-1)),
        ):
            copy.start()
            s2.append(copy)
    for j in range(per_class):
        copy = handed(block(j))
        copy.start()
        handovers.append(copy)

    for k in range(3):
        e_copies[k].wait_recv()
    carried = reach[1] * incoming[0]
    for k in (1, 2):
        reached = jnp.where(before[0] == before[k], reach[k + 1], 0.0)
        carried = carried + reached * jnp.exp(-float(ROWS * k) * rate) * incoming[k]
    carried = jnp.exp(-(CENTER + 1.0) * rate) * carried + change_zero
    entering = jnp.zeros((ROWS, 128), F32)
    changed = jnp.zeros((ROWS, 128), F32)
    for g in range(PAIRS):
        lanes = slice(128 * g, 128 * g + 128)
        entering = entering + growth[:, lanes] * carried[g : g + 1, :]
        changed = changed + growth[:, lanes] * change_one[g : g + 1, :]
    total = total + survives[...] * (entering + jnp.where(down >= 1.0, changed, 0.0))
    total = total + pltpu.roll(total, CH, 1)
    skips = jnp.concatenate([skip[...], skip[...]], axis=1)
    gated = query[...] * (total + skips * product[...])
    side = is_low(QUARTER)
    for h in range(2):
        top = gated[HALF * h : HALF * h + QUARTER, :]
        bottom = gated[HALF * h + QUARTER : HALF * (h + 1), :]
        a_send[h] = jnp.where(side, top, bottom).astype(BF16)

    a_copies = []

    def gather(i, there, target):
        copy = pltpu.make_async_remote_copy(
            src_ref=a_send.at[target],
            dst_ref=a_recv.at[c * nx + x],
            send_sem=as_sem.at[i],
            recv_sem=ar_sem.at[c * nx + x],
            device_id=(y, z, there, target),
            device_id_type=MESH,
        )
        copy.start()
        a_copies.append(copy)

    for i, d in enumerate(distances(nx)):
        there = lax.rem(x + d, nx)
        gather(2 * i, there, c)
        gather(2 * i + 1, there, other)
    gather(2 * nx - 2, x, other)
    a_recv[c * nx + x] = a_send[c]

    def arrived(index, sem):
        pltpu.make_async_copy(
            wout.at[parity, columns(index)], wout.at[parity, columns(index)], s2_recv.at[sem]
        ).wait()

    def hand(index):
        copy = handed(index)
        copy.start()
        handovers.append(copy)

    far = 2 * per_class
    for j in range(half_class):
        k = j + half_class
        arrived(block(j, -1), j)
        copy = passed_on(block(j, -1), far + j, at_y(1))
        copy.start()
        s2.append(copy)
        arrived(block(k, 1), per_class + k)
        copy = passed_on(block(k, 1), far + k, at_y(-1))
        copy.start()
        s2.append(copy)
        hand(block(j, -1))
        hand(block(k, 1))
    for j in range(half_class):
        k = j + half_class
        arrived(block(k, -1), k)
        hand(block(k, -1))
        arrived(block(j, 1), per_class + j)
        hand(block(j, 1))

    for d in range(1, 2 * nx):
        sender = lax.rem(c * nx + x + d, 2 * nx)
        pltpu.make_async_copy(a_recv.at[0], a_recv.at[0], ar_sem.at[sender]).wait()
    for m in range(nx):
        left = a_recv[2 * m].astype(F32)
        right = a_recv[2 * m + 1].astype(F32)
        lanes = slice(128 * m, 128 * m + 128)
        lhs[0:QUARTER, lanes] = jnp.where(side, left, pltpu.roll(right, CH, 1)).astype(BF16)
        lhs[QUARTER:HALF, lanes] = jnp.where(side, pltpu.roll(left, CH, 1), right).astype(BF16)

    for j in range(half_class):
        k = j + half_class
        arrived(block(j, 2), far + j)
        hand(block(j, 2))
        arrived(block(k, 2), far + k)
        hand(block(k, 2))
    partner = pl.ds(pl.multiple_of(other * group, group), group)
    for index in range(nz):
        pltpu.make_async_copy(
            wout.at[partner, columns(index)], wout.at[partner, columns(index)], oc_recv.at[index]
        ).wait()

    c_copies = []

    def scatter(i, slot, there, target):
        copy = pltpu.make_async_remote_copy(
            src_ref=c_send.at[slot, target],
            dst_ref=c_recv.at[c * nz + z],
            send_sem=cs_sem.at[i],
            recv_sem=cr_sem.at[c * nz + z],
            device_id=(y, there, x, target),
            device_id_type=MESH,
        )
        copy.start()
        c_copies.append(copy)

    for i, d in enumerate([*distances(nz), 0]):
        there = lax.rem(z + d, nz)
        sums = jnp.dot(lhs[...], wout[:, columns(there)], preferred_element_type=F32)
        top, bottom = sums[0:QUARTER, :], sums[QUARTER:HALF, :]
        c_send[i, 0] = jnp.where(side, top, pltpu.roll(bottom, CH, 1)).astype(BF16)
        c_send[i, 1] = jnp.where(side, pltpu.roll(top, CH, 1), bottom).astype(BF16)
        if d:
            scatter(2 * i, i, there, c)
            scatter(2 * i + 1, i, there, other)
        else:
            scatter(2 * i, i, there, other)
            c_recv[c * nz + z] = c_send[i, c]
    for d in range(1, 2 * nz):
        sender = lax.rem(c * nz + z + d, 2 * nz)
        pltpu.make_async_copy(c_recv.at[0], c_recv.at[0], cr_sem.at[sender]).wait()
    pieces = []
    for h in range(2):
        added = c_recv[h * nz].astype(F32)
        for k in range(1, nz):
            added = added + c_recv[h * nz + k].astype(F32)
        pieces += [added, pltpu.roll(added, CH, 1)]
    result = jnp.concatenate(pieces, axis=0)
    out[...] = result.T[0:CH, :].astype(BF16)

    for copy in (*s1, *s2, *handovers, *e_copies, *a_copies, *c_copies):
        copy.wait_send()
    halo_copy.wait_send()


def local(
    sizes,
    tokens, norm_gain, in_weight, short_filter, rates, residues, skip, out_weight, segment_ids,
):
    ny, nz, nx = sizes
    width = tokens.shape[1]
    turned = jnp.transpose(in_weight, (1, 2, 0)).reshape(3 * CH, width)
    per_class = nz // CLASSES
    vmem, hbm = pl.BlockSpec(memory_space=pltpu.VMEM), pl.BlockSpec(memory_space=pl.ANY)
    dma = pltpu.SemaphoreType.DMA
    result = pl.pallas_call(
        functools.partial(kernel, sizes),
        out_shape=jax.ShapeDtypeStruct((CH, ROWS), BF16),
        in_specs=[hbm, vmem, hbm, vmem, vmem, vmem, vmem, hbm, vmem],
        out_specs=vmem,
        scratch_shapes=[
            pltpu.VMEM((ROWS, WIDTH), BF16),
            pltpu.VMEM((4 * CH, WIDTH), BF16),
            pltpu.VMEM((2 * nx * CH, nz * 128), BF16),
            pltpu.VMEM((ROWS + 8, 256), F32),
            pltpu.VMEM((8, 256), F32),
            pltpu.VMEM((ROWS, PAIRS * 128), F32),
            pltpu.VMEM((2 * ROWS, PAIRS * 128), BF16),
            pltpu.VMEM((ROWS, 2 * ROWS), BF16),
            pltpu.VMEM((ROWS, 128), F32),
            pltpu.VMEM((ROWS, 128), F32),
            pltpu.VMEM((ROWS, 256), F32),
            pltpu.VMEM((ROWS, 128), F32),
            pltpu.VMEM((ROWS, 128), F32),
            pltpu.VMEM((ROWS, 128), F32),
            pltpu.VMEM((PAIRS, 128), F32),
            pltpu.VMEM((3, PAIRS, 128), F32),
            pltpu.VMEM((2, QUARTER, 128), BF16),
            pltpu.VMEM((2 * nx, QUARTER, 128), BF16),
            pltpu.VMEM((HALF, nx * 128), BF16),
            pltpu.VMEM((nz, 2, QUARTER, 128), BF16),
            pltpu.VMEM((2 * nz, QUARTER, 128), BF16),
            dma((WIDTH // TOKEN_CHUNK,)),
            dma((2 * WIDTH // WEIGHT_CHUNK,)),
            dma((per_class * nx,)),
            dma((per_class * nx,)),
            dma((3 * per_class,)),
            dma((3 * per_class,)),
            dma((nz,)),
            dma((nz,)),
            dma((2,)),
            dma((3,)),
            dma((3,)),
            dma((2 * nx,)),
            dma((2 * nx,)),
            dma((2 * nz,)),
            dma((2 * nz,)),
        ],
        compiler_params=pltpu.CompilerParams(
            collective_id=0, has_side_effects=True, vmem_limit_bytes=60 * 1024 * 1024
        ),
    )(
        tokens,
        norm_gain.reshape(1, width),
        turned,
        short_filter,
        rates,
        residues,
        skip.reshape(1, CH),
        out_weight,
        segment_ids.reshape(-1, 128),
    )
    return result.T


def solution(mesh):
    ny = mesh.shape["ctx"]
    nz, nx = 8, 8
    torus = Mesh(mesh.devices.reshape(ny, nz, nx, 2), ("ctx", *MP))
    placed = (
        P("ctx", None),
        P(),
        P(None, None, MP),
        P(None, None, MP),
        P(None, MP),
        P(None, MP),
        P(MP),
        P(MP, None),
        P(),
    )
    return jax.shard_map(
        functools.partial(local, (ny, nz, nx)),
        mesh=torus,
        in_specs=placed,
        out_specs=P("ctx", MP),
        check_vma=False,
    )
```

time: 210 us -> 54.2 us (0.26)
  the two profiles are of different devices: /device:TPU:2 before, /device:TPU:1 now
where the time goes in v1:
time: 54.2 us; the launch traced here: 53.9 us
  Pallas kernels  52.5 us (97%)
  local copies, waits for them, and re-layouts  1.38 us (3%)
    pallas_call x1, Pallas kernels, local(): pl.pallas_call(functools.partial(kernel, sizes), out_shape=jax.ShapeDtype...  52.5 us
    unnamed x1, local copies, waits for them, and re-layouts  1.38 us

profile of v1, /device:TPU:1, one launch (start us, length us, event | category | flops | bytes accessed | tf_op | source)
XLA Modules:
  0.0 53.9 jit_solution(18311646387325886277)
XLA Ops:
  0.0 52.5 %shard_map.91 = bf16[64,192]{1,0:T(8,128)(2,1)} custom-call(bf16[192,8192]{1,0:T(8,128)(2,1)} %tokens.1, f32[1,8192]{1,0:T(1,128)} %bitcast.9, bf16[192,8192]{1,0:T(8,128)(2,1)} %bitcast.7, f32[3,3,64]{2,1,0:T(4,128)} %taps.1, f32[16,64]{1,0:T(8,128)} %rates.1, f32[16,64]{1,0:T(8,128)} %residues.1, f32[1,64]{1,0:T(1,128)} %bitcast.11, ...), custom_call_target="tpu_custom_call" | custom-call | tf_op jit(solution)/shard_map/pallas_call | solution.py:452
  52.5 1.4 %copy.11 = bf16[192,64]{0,1:T(8,128)(2,1)} copy(bf16[192,64]{0,1:T(8,128)(2,1)} %bitcast.8) | data formatting | bytes 49152

commit v2 on v1

v2 whole, which is shorter than its diff:
```python
import functools

import jax
import jax.numpy as jnp
from jax import lax
from jax.experimental import pallas as pl
from jax.experimental.pallas import tpu as pltpu
from jax.sharding import Mesh
from jax.sharding import PartitionSpec as P

MP = ("mp_0", "mp_1", "mp_2")
MESH = pl.DeviceIdType.MESH
F32 = jnp.float32
BF16 = jnp.bfloat16

epsilon = 1e-06

ROWS = 192
HALF = ROWS // 2
QUARTER = HALF // 2
CH = 64
POLES = 16
PAIRS = POLES // 2
WIDTH = 8192
DOCS = 8
CENTER = float(ROWS // 2)
REACH = 3
EARLY = 2
TOKEN_CHUNK = 2048
WEIGHT_CHUNK = 1024


def distances(count):
    return sorted(range(1, count), key=lambda d: -min(d, count - d))


def kernel(
    sizes,
    tokens, gain_in, in_weight, taps_in, rates_in, residues_in, skip_in, out_weight, ids_in,
    out,
    gain, taps, rates, residues, skip, ids, small_sem,
    tok, win, wout, proj, halo, growth, weighted, visible, product, query, acc,
    lag_one, lag_two, survives, ends, incoming, a_send, a_recv, lhs, sums, c_send, c_recv,
    tok_sem, win_sem, s1_send, s1_recv, s2_send, s2_recv, oc_send, oc_recv,
    halo_sem, e_send, e_recv, as_sem, ar_sem, cs_sem, cr_sem, z_ready,
):
    ny, nz, nx = sizes
    y, z, x, c = (lax.axis_index(name) for name in ("ctx", *MP))
    other = 1 - c
    def at_y(step):
        return (lax.rem(y + step + ny, ny), z, x, c)

    small = [
        pltpu.make_async_copy(source, target, small_sem.at[k])
        for k, (source, target) in enumerate(
            (
                (ids_in, ids),
                (rates_in, rates),
                (residues_in, residues),
                (taps_in, taps),
                (skip_in, skip),
                (gain_in, gain),
            )
        )
    ]
    for load in small:
        load.start()
    tok_loads = []
    for k in range(WIDTH // TOKEN_CHUNK):
        span = pl.ds(k * TOKEN_CHUNK, TOKEN_CHUNK)
        load = pltpu.make_async_copy(tokens.at[:, span], tok.at[:, span], tok_sem.at[k])
        load.start()
        tok_loads.append(load)

    barrier = pltpu.get_barrier_semaphore()
    greeted = [(y, z, x, other)]
    for side in (c, other):
        greeted += [(y, z, lax.rem(x + d, nx), side) for d in range(1, nx)]
    steps = sorted({d % ny for k in range(1, REACH + 1) for d in (k, -k)})
    greeted += [at_y(d) for d in steps]
    for device in greeted:
        pl.semaphore_signal(barrier, inc=1, device_id=device, device_id_type=MESH)
    for d in range(1, nz):

        @pl.when(z + d < nz)
        def _():
            for side in (c, other):
                target = (y, z + d, x, side)
                pl.semaphore_signal(barrier, inc=1, device_id=target, device_id_type=MESH)

    win_loads = []
    for k in range(WIDTH // WEIGHT_CHUNK):
        span = pl.ds(k * WEIGHT_CHUNK, WEIGHT_CHUNK)
        load = pltpu.make_async_copy(in_weight.at[:, span], win.at[:, span], win_sem.at[k])
        load.start()
        win_loads.append(load)
    for load in small:
        load.wait()

    id_values = ids[...].astype(F32)
    bounds = [
        jnp.sum(jnp.where(id_values < float(k), 1.0, 0.0), axis=(0, 1), keepdims=True)
        for k in range(1, DOCS)
    ]

    def document(position):
        total = jnp.zeros_like(position)
        for bound in bounds:
            total = total + jnp.where(position >= bound, 1.0, 0.0)
        return total

    base = (y * ROWS).astype(F32)
    down = lax.broadcasted_iota(jnp.int32, (ROWS, 128), 0).astype(F32)
    own = document(down + base)

    def document_at(offset):
        return document(jnp.zeros((1, 128), F32) + (base + float(offset)))

    before = [document_at(-1 - ROWS * k) for k in range(3)]
    reach = [jnp.where(y >= k, 1.0, 0.0).astype(F32) for k in range(4)]
    survives[...] = jnp.where(own == before[0], reach[1], 0.0)
    lag_one[...] = jnp.where(own == document(down + (base - 1.0)), 1.0, 0.0)
    lag_two[...] = jnp.where(own == document(down + (base - 2.0)), 1.0, 0.0)
    whole = jnp.where(document_at(0) == document_at(ROWS - 1), 1.0, 0.0)
    across = lax.broadcasted_iota(jnp.int32, (1, 2 * ROWS), 1).astype(F32)
    across = jnp.where(across < float(ROWS), across, across - float(ROWS))
    beside = document(across + base)
    seen = (down[:, :1] >= across) & (own[:, :1] == beside)
    visible[...] = jnp.where(seen, 1.0, 0.0).astype(BF16)

    def paired(ref):
        return jnp.concatenate([ref[0:PAIRS, :], ref[PAIRS:POLES, :]], axis=1)

    rate = paired(rates)
    twice = -2.0 * rate
    small = twice * (1.0 + twice * (0.5 + twice * (1.0 / 6.0 + twice * (1.0 / 24.0 + twice * (
        1.0 / 120.0)))))
    weight = paired(residues) * jnp.sqrt(-small)

    squares = jnp.zeros((ROWS, 128), F32)
    for k in range(WIDTH // TOKEN_CHUNK):
        tok_loads[k].wait()
        for lane in range(k * TOKEN_CHUNK, (k + 1) * TOKEN_CHUNK, 128):
            piece = tok[:, lane : lane + 128].astype(F32)
            squares = squares + piece * piece
    mean_square = jnp.sum(squares, axis=1, keepdims=True) * (1.0 / WIDTH)
    scale = lax.rsqrt(mean_square + epsilon)

    pl.semaphore_wait(barrier, len(greeted) + 2 * z)
    for d in range(1, nz):

        @pl.when(z - d >= 0)
        def _():
            for side in (c, other):
                target = (y, z - d, x, side)
                pl.semaphore_signal(
                    z_ready.at[c * nz + z], inc=1, device_id=target, device_id_type=MESH
                )

    mine = pl.ds(pl.multiple_of(c * CH, CH), CH)
    partner = pl.ds(pl.multiple_of(other * CH, CH), CH)

    width = nx * 128 // 2
    kind = lax.rem(y, 2)

    def columns(there, half):
        return pl.ds(pl.multiple_of((2 * there + half) * width, width), width)

    def place(index, half):
        return wout.at[index, mine, columns(0, half)]

    def spread(there):
        return pltpu.make_async_remote_copy(
            src_ref=out_weight.at[:, columns(there, kind)],
            dst_ref=place(z, kind),
            send_sem=s1_send.at[there],
            recv_sem=s1_recv.at[z],
            device_id=(y, there, x, c),
            device_id_type=MESH,
        )

    for half, sem in ((kind, s1_recv), (1 - kind, s2_recv)):
        pltpu.make_async_copy(
            out_weight.at[:, columns(z, half)], place(z, half), sem.at[z]
        ).start()
    for d in range(nz - 1, 0, -1):

        @pl.when(z - d >= 0)
        def _():
            spread(z - d).start()

    def wait_z(there, side):
        pl.semaphore_wait(z_ready.at[side * nz + there], 1)

    def spread_later(d):
        @pl.when(z + d < nz)
        def _():
            wait_z(z + d, c)
            spread(z + d).start()

    acc[...] = jnp.zeros_like(acc)
    for k in range(WIDTH // WEIGHT_CHUNK):
        win_loads[k].wait()
        span = pl.ds(k * WEIGHT_CHUNK, WEIGHT_CHUNK)
        normed = (tok[:, span].astype(F32) * scale * gain[:, span]).astype(BF16)
        acc[...] += lax.dot_general(
            normed, win[:, span], (((1,), (1,)), ((), ())), preferred_element_type=F32
        )
    proj[0:8, :] = jnp.zeros((8, 256), F32)
    rounded = acc[...].astype(BF16).astype(F32)
    proj[8 : 8 + ROWS, 0:128] = rounded[:, 0:128]
    value_part = rounded[:, 128 : 3 * CH]
    proj[8 : 8 + ROWS, 128:256] = jnp.concatenate([value_part, value_part], axis=1)
    halo_copy = pltpu.make_async_remote_copy(
        src_ref=proj.at[pl.ds(ROWS, 8)],
        dst_ref=halo,
        send_sem=halo_sem.at[0],
        recv_sem=halo_sem.at[1],
        device_id=at_y(1),
        device_id_type=MESH,
    )
    halo_copy.start()

    for d in range(1, EARLY + 1):
        spread_later(d)

    def is_low(count):
        return lax.broadcasted_iota(jnp.int32, (count, 128), 1) < CH

    tap_rows = []
    for j in range(3):
        first = jnp.concatenate([taps[j, 0:1, :], taps[j, 1:2, :]], axis=1)
        second = jnp.concatenate([taps[j, 2:3, :], taps[j, 2:3, :]], axis=1)
        tap_rows.append((first, second))

    def filtered(count):
        tiles = []
        for side in range(2):
            lanes = slice(128 * side, 128 * side + 128)
            total = tap_rows[0][side] * proj[8 : 8 + count, lanes]
            total = total + tap_rows[1][side] * (proj[7 : 7 + count, lanes] * lag_one[0:count, :])
            total = total + tap_rows[2][side] * (proj[6 : 6 + count, lanes] * lag_two[0:count, :])
            tiles.append(total)
        turned = pltpu.roll(tiles[0], CH, 1)
        side = is_low(count)
        return jnp.where(side, tiles[0], turned), jnp.where(side, turned, tiles[0]) * tiles[1]

    query_part, product_part = filtered(ROWS)
    query[...] = query_part
    product[...] = product_part

    offset = down - CENTER
    for g in range(PAIRS):
        lanes = slice(128 * g, 128 * g + 128)
        exponent = offset * rate[g : g + 1, :]
        value = jnp.exp(exponent) * product_part
        high = value.astype(BF16)
        weighted[0:ROWS, lanes] = high
        weighted[ROWS : 2 * ROWS, lanes] = (value - high.astype(F32)).astype(BF16)
        growth[:, lanes] = weight[g : g + 1, :] * jnp.exp(-exponent)
    last = []
    total = jnp.zeros((ROWS, 128), F32)
    for g in range(PAIRS):
        lanes = slice(128 * g, 128 * g + 128)
        inside = jnp.dot(visible[...], weighted[:, lanes], preferred_element_type=F32)
        last.append(inside[ROWS - 1 : ROWS, :])
        total = total + growth[:, lanes] * inside
    last = jnp.concatenate(last, axis=0)

    halo_copy.wait_recv()
    proj[0:8, :] = halo[...] * reach[1]
    query_top, product_top = filtered(8)
    change = product_top - product[0:8, :]
    query[0:8, :] = query_top
    product[0:8, :] = product_top
    change_zero = jnp.exp(-CENTER * rate) * change[0:1, :]
    change_one = jnp.exp((1.0 - CENTER) * rate) * change[1:2, :]
    ends[...] = jnp.exp((CENTER + 1.0 - ROWS) * rate) * (
        last + whole * (change_zero + change_one)
    )
    e_copies = []
    for k in range(3):
        copy = pltpu.make_async_remote_copy(
            src_ref=ends,
            dst_ref=incoming.at[k],
            send_sem=e_send.at[k],
            recv_sem=e_recv.at[k],
            device_id=at_y(k + 1),
            device_id_type=MESH,
        )
        copy.start()
        e_copies.append(copy)

    spread_later(EARLY + 1)

    for k in range(3):
        e_copies[k].wait_recv()
    carried = reach[1] * incoming[0]
    for k in (1, 2):
        reached = jnp.where(before[0] == before[k], reach[k + 1], 0.0)
        carried = carried + reached * jnp.exp(-float(ROWS * k) * rate) * incoming[k]
    carried = jnp.exp(-(CENTER + 1.0) * rate) * carried + change_zero
    entering = jnp.zeros((ROWS, 128), F32)
    changed = jnp.zeros((ROWS, 128), F32)
    for g in range(PAIRS):
        lanes = slice(128 * g, 128 * g + 128)
        entering = entering + growth[:, lanes] * carried[g : g + 1, :]
        changed = changed + growth[:, lanes] * change_one[g : g + 1, :]
    total = total + survives[...] * (entering + jnp.where(down >= 1.0, changed, 0.0))
    total = total + pltpu.roll(total, CH, 1)
    skips = jnp.concatenate([skip[...], skip[...]], axis=1)
    gated = query[...] * (total + skips * product[...])
    side = is_low(QUARTER)
    for h in range(2):
        top = gated[HALF * h : HALF * h + QUARTER, :]
        bottom = gated[HALF * h + QUARTER : HALF * (h + 1), :]
        a_send[h] = jnp.where(side, top, bottom).astype(BF16)

    def gather(there, target):
        return pltpu.make_async_remote_copy(
            src_ref=a_send.at[target],
            dst_ref=a_recv.at[c * nz + z],
            send_sem=as_sem.at[target * nz + there],
            recv_sem=ar_sem.at[c * nz + z],
            device_id=(y, there, x, target),
            device_id_type=MESH,
        )

    for d in range(nz - 1, 0, -1):

        @pl.when(z - d >= 0)
        def _():
            gather(z - d, c).start()
            gather(z - d, other).start()

    gather(z, other).start()
    a_recv[c * nz + z] = a_send[c]
    for d in range(1, nz):

        @pl.when(z + d < nz)
        def _():
            if d > EARLY + 1:
                wait_z(z + d, c)
            gather(z + d, c).start()
            wait_z(z + d, other)
            gather(z + d, other).start()
            if d > EARLY + 1:
                spread(z + d).start()

    def forwarded(index):
        return pltpu.make_async_remote_copy(
            src_ref=place(index, kind),
            dst_ref=place(index, kind),
            send_sem=s2_send.at[index],
            recv_sem=s2_recv.at[index],
            device_id=at_y(-1 if index % 2 else 1),
            device_id_type=MESH,
        )

    def handed(index, half):
        return pltpu.make_async_remote_copy(
            src_ref=place(index, half),
            dst_ref=place(index, half),
            send_sem=oc_send.at[2 * index + half],
            recv_sem=oc_recv.at[2 * index + half],
            device_id=(y, z, x, other),
            device_id_type=MESH,
        )

    for k in range(nz):
        pltpu.make_async_copy(place(k, kind), place(k, kind), s1_recv.at[k]).wait()

        @pl.when(z != k)
        def _():
            forwarded(k).start()

        handed(k, kind).start()
    for k in range(nz):
        pltpu.make_async_copy(place(k, 1 - kind), place(k, 1 - kind), s2_recv.at[k]).wait()
        handed(k, 1 - kind).start()

    for k in range(nz):
        for half in range(2):
            piece = wout.at[k, partner, columns(0, half)]
            pltpu.make_async_copy(piece, piece, oc_recv.at[2 * k + half]).wait()
        for h in range(2):

            @pl.when((z != k) | (c != h))
            def _():
                slot = a_recv.at[h * nz + k]
                pltpu.make_async_copy(slot, slot, ar_sem.at[h * nz + k]).wait()

        left = a_recv[k].astype(F32)
        right = a_recv[nz + k].astype(F32)
        lhs[0:QUARTER, :] = jnp.where(side, left, pltpu.roll(right, CH, 1)).astype(BF16)
        lhs[QUARTER:HALF, :] = jnp.where(side, pltpu.roll(left, CH, 1), right).astype(BF16)
        term = jnp.dot(lhs[...], wout[k], preferred_element_type=F32)
        sums[...] = term if k == 0 else sums[...] + term

    def scatter(slot, there, target):
        return pltpu.make_async_remote_copy(
            src_ref=c_send.at[slot, target],
            dst_ref=c_recv.at[c * nx + x],
            send_sem=cs_sem.at[2 * slot + target],
            recv_sem=cr_sem.at[c * nx + x],
            device_id=(y, z, there, target),
            device_id_type=MESH,
        )

    c_copies = []
    for i, d in enumerate([*distances(nx), 0]):
        there = lax.rem(x + d, nx)
        block = sums[:, pl.ds(pl.multiple_of(there * 128, 128), 128)]
        top, bottom = block[0:QUARTER, :], block[QUARTER:HALF, :]
        c_send[i, 0] = jnp.where(side, top, pltpu.roll(bottom, CH, 1)).astype(BF16)
        c_send[i, 1] = jnp.where(side, pltpu.roll(top, CH, 1), bottom).astype(BF16)
        for target in (c, other) if d else (other,):
            copy = scatter(i, there, target)
            copy.start()
            c_copies.append(copy)
    c_recv[c * nx + x] = c_send[nx - 1, c]
    for d in range(1, 2 * nx):
        sender = lax.rem(c * nx + x + d, 2 * nx)
        pltpu.make_async_copy(c_recv.at[0], c_recv.at[0], cr_sem.at[sender]).wait()
    pieces = []
    for h in range(2):
        added = c_recv[h * nx].astype(F32)
        for k in range(1, nx):
            added = added + c_recv[h * nx + k].astype(F32)
        pieces += [added, pltpu.roll(added, CH, 1)]
    result = jnp.concatenate(pieces, axis=0)
    out[...] = result.T[0:CH, :].astype(BF16)

    for copy in (*e_copies, *c_copies, halo_copy, gather(z, other)):
        copy.wait_send()
    for k in range(nz):
        handed(k, 0).wait_send()
        handed(k, 1).wait_send()

        @pl.when(z != k)
        def _():
            spread(k).wait_send()
            forwarded(k).wait_send()
            gather(k, c).wait_send()
            gather(k, other).wait_send()


def local(
    sizes,
    tokens, norm_gain, in_weight, short_filter, rates, residues, skip, out_weight, segment_ids,
):
    ny, nz, nx = sizes
    width = tokens.shape[1]
    turned = jnp.transpose(in_weight, (1, 2, 0)).reshape(3 * CH, width)
    vmem, hbm = pl.BlockSpec(memory_space=pltpu.VMEM), pl.BlockSpec(memory_space=pl.ANY)
    dma = pltpu.SemaphoreType.DMA
    result = pl.pallas_call(
        functools.partial(kernel, sizes),
        out_shape=jax.ShapeDtypeStruct((CH, ROWS), BF16),
        in_specs=[hbm] * 9,
        out_specs=vmem,
        scratch_shapes=[
            pltpu.VMEM((1, WIDTH), F32),
            pltpu.VMEM(short_filter.shape, F32),
            pltpu.VMEM(rates.shape, F32),
            pltpu.VMEM(residues.shape, F32),
            pltpu.VMEM((1, CH), F32),
            pltpu.VMEM((segment_ids.shape[0] // 128, 128), jnp.int32),
            dma((6,)),
            pltpu.VMEM((ROWS, WIDTH), BF16),
            pltpu.VMEM((3 * CH, WIDTH), BF16),
            pltpu.VMEM((nz, 2 * CH, nx * 128), BF16),
            pltpu.VMEM((ROWS + 8, 256), F32),
            pltpu.VMEM((8, 256), F32),
            pltpu.VMEM((ROWS, PAIRS * 128), F32),
            pltpu.VMEM((2 * ROWS, PAIRS * 128), BF16),
            pltpu.VMEM((ROWS, 2 * ROWS), BF16),
            pltpu.VMEM((ROWS, 128), F32),
            pltpu.VMEM((ROWS, 128), F32),
            pltpu.VMEM((ROWS, 3 * CH), F32),
            pltpu.VMEM((ROWS, 128), F32),
            pltpu.VMEM((ROWS, 128), F32),
            pltpu.VMEM((ROWS, 128), F32),
            pltpu.VMEM((PAIRS, 128), F32),
            pltpu.VMEM((3, PAIRS, 128), F32),
            pltpu.VMEM((2, QUARTER, 128), BF16),
            pltpu.VMEM((2 * nz, QUARTER, 128), BF16),
            pltpu.VMEM((HALF, 2 * CH), BF16),
            pltpu.VMEM((HALF, nx * 128), F32),
            pltpu.VMEM((nx, 2, QUARTER, 128), BF16),
            pltpu.VMEM((2 * nx, QUARTER, 128), BF16),
            dma((WIDTH // TOKEN_CHUNK,)),
            dma((WIDTH // WEIGHT_CHUNK,)),
            dma((nz,)),
            dma((nz,)),
            dma((nz,)),
            dma((nz,)),
            dma((2 * nz,)),
            dma((2 * nz,)),
            dma((2,)),
            dma((3,)),
            dma((3,)),
            dma((2 * nz,)),
            dma((2 * nz,)),
            dma((2 * nx,)),
            dma((2 * nx,)),
            pltpu.SemaphoreType.REGULAR((2 * nz,)),
        ],
        compiler_params=pltpu.CompilerParams(
            collective_id=0, has_side_effects=True, vmem_limit_bytes=60 * 1024 * 1024
        ),
    )(
        tokens,
        norm_gain.reshape(1, width),
        turned,
        short_filter,
        rates,
        residues,
        skip.reshape(1, CH),
        out_weight,
        segment_ids.reshape(-1, 128),
    )
    return result.T


def solution(mesh):
    ny = mesh.shape["ctx"]
    nz, nx = 8, 8
    torus = Mesh(mesh.devices.reshape(ny, nz, nx, 2), ("ctx", *MP))
    placed = (
        P("ctx", None),
        P(),
        P(None, None, MP),
        P(None, None, MP),
        P(None, MP),
        P(None, MP),
        P(MP),
        P(MP, None),
        P(),
    )
    return jax.shard_map(
        functools.partial(local, (ny, nz, nx)),
        mesh=torus,
        in_specs=placed,
        out_specs=P("ctx", MP),
        check_vma=False,
    )
```

time: 54.2 us -> 48.5 us (0.89)
  Pallas kernels: 52.5 us -> 46.9 us
    pallas_call x1, Pallas kernels: 52.5 us -> 46.9 us  [local(): pl.pallas_call(functools.partial(kernel, sizes), out_shape=jax.ShapeDtype...]
where the time goes in v2:
time: 48.5 us; the launch traced here: 48.3 us
  Pallas kernels  46.9 us (97%)
  local copies, waits for them, and re-layouts  1.38 us (3%)
    pallas_call x1, Pallas kernels, local(): pl.pallas_call(functools.partial(kernel, sizes), out_shape=jax.ShapeDtype...  46.9 us
    unnamed x1, local copies, waits for them, and re-layouts  1.38 us

profile of v2, /device:TPU:1, one launch (start us, length us, event | category | flops | bytes accessed | tf_op | source)
XLA Modules:
  0.0 48.3 jit_solution(17666013220281378827)
XLA Ops:
  0.0 46.9 %shard_map.91 = bf16[64,192]{1,0:T(8,128)(2,1)} custom-call(bf16[192,8192]{1,0:T(8,128)(2,1)} %tokens.1, f32[1,8192]{1,0:T(1,128)} %bitcast.9, bf16[192,8192]{1,0:T(8,128)(2,1)} %bitcast.7, f32[3,3,64]{2,1,0:T(4,128)} %taps_in.1, f32[16,64]{1,0:T(8,128)} %rates_in.1, f32[16,64]{1,0:T(8,128)} %residues_in.1, f32[1,64]{1,0:T(1,128)} %bitcast.11, ...), custom_call_target="tpu_custom_call" | custom-call | tf_op jit(solution)/shard_map/pallas_call | solution.py:457
  46.9 1.4 %copy.11 = bf16[192,64]{0,1:T(8,128)(2,1)} copy(bf16[192,64]{0,1:T(8,128)(2,1)} %bitcast.8) | data formatting | bytes 49152

commit v3 on v2

--- a/solution.py
+++ b/solution.py
@@ -25,6 +25,7 @@
 DOCS = 8
 CENTER = float(ROWS // 2)
 REACH = 3
+SHARES = 4
 EARLY = 2
 TOKEN_CHUNK = 2048
 WEIGHT_CHUNK = 1024
@@ -50,6 +51,9 @@
     def at_y(step):
         return (lax.rem(y + step + ny, ny), z, x, c)
 
+    def waited(ref, sem):
+        pltpu.make_async_copy(ref, ref, sem).wait()
+
     small = [
         pltpu.make_async_copy(source, target, small_sem.at[k])
         for k, (source, target) in enumerate(
@@ -160,28 +164,34 @@
     mine = pl.ds(pl.multiple_of(c * CH, CH), CH)
     partner = pl.ds(pl.multiple_of(other * CH, CH), CH)
 
-    width = nx * 128 // 2
-    kind = lax.rem(y, 2)
-
-    def columns(there, half):
-        return pl.ds(pl.multiple_of((2 * there + half) * width, width), width)
-
-    def place(index, half):
-        return wout.at[index, mine, columns(0, half)]
+    width = nx * 128 // SHARES
+    kind = lax.rem(y, SHARES)
+
+    def columns(there, part):
+        return pl.ds(pl.multiple_of((SHARES * there + part) * width, width), width)
+
+    def share(turned):
+        return lax.rem(kind + turned + SHARES, SHARES)
+
+    def place(index, part):
+        return wout.at[index, mine, columns(0, part)]
 
     def spread(there):
         return pltpu.make_async_remote_copy(
             src_ref=out_weight.at[:, columns(there, kind)],
             dst_ref=place(z, kind),
-            send_sem=s1_send.at[there],
+            send_sem=s1_send,
             recv_sem=s1_recv.at[z],
             device_id=(y, there, x, c),
             device_id_type=MESH,
         )
 
-    for half, sem in ((kind, s1_recv), (1 - kind, s2_recv)):
+    left_in, right_in, far_in = (s2_recv.at[k] for k in range(3))
+    for part, sem in (
+        (kind, s1_recv), (share(-1), left_in), (share(1), right_in), (share(2), far_in)
+    ):
         pltpu.make_async_copy(
-            out_weight.at[:, columns(z, half)], place(z, half), sem.at[z]
+            out_weight.at[:, columns(z, part)], place(z, part), sem.at[z]
         ).start()
     for d in range(nz - 1, 0, -1):
 
@@ -320,7 +330,7 @@
         return pltpu.make_async_remote_copy(
             src_ref=a_send.at[target],
             dst_ref=a_recv.at[c * nz + z],
-            send_sem=as_sem.at[target * nz + there],
+            send_sem=as_sem,
             recv_sem=ar_sem.at[c * nz + z],
             device_id=(y, there, x, target),
             device_id_type=MESH,
@@ -347,42 +357,34 @@
             if d > EARLY + 1:
                 spread(z + d).start()
 
-    def forwarded(index):
+    def forwarded(index, part, route):
         return pltpu.make_async_remote_copy(
-            src_ref=place(index, kind),
-            dst_ref=place(index, kind),
-            send_sem=s2_send.at[index],
-            recv_sem=s2_recv.at[index],
-            device_id=at_y(-1 if index % 2 else 1),
+            src_ref=place(index, part),
+            dst_ref=place(index, part),
+            send_sem=s2_send,
+            recv_sem=s2_recv.at[route, index],
+            device_id=at_y(-1 if route == 1 or (route == 2 and index % 2) else 1),
             device_id_type=MESH,
         )
 
-    def handed(index, half):
+    def relayed(index):
+        return forwarded(index, share(1 if index % 2 else -1), 2)
+
+    def handed(index, part):
         return pltpu.make_async_remote_copy(
-            src_ref=place(index, half),
-            dst_ref=place(index, half),
-            send_sem=oc_send.at[2 * index + half],
-            recv_sem=oc_recv.at[2 * index + half],
+            src_ref=place(index, part),
+            dst_ref=place(index, part),
+            send_sem=oc_send,
+            recv_sem=oc_recv.at[index],
             device_id=(y, z, x, other),
             device_id_type=MESH,
         )
 
-    for k in range(nz):
-        pltpu.make_async_copy(place(k, kind), place(k, kind), s1_recv.at[k]).wait()
-
-        @pl.when(z != k)
-        def _():
-            forwarded(k).start()
-
-        handed(k, kind).start()
-    for k in range(nz):
-        pltpu.make_async_copy(place(k, 1 - kind), place(k, 1 - kind), s2_recv.at[k]).wait()
-        handed(k, 1 - kind).start()
-
-    for k in range(nz):
-        for half in range(2):
-            piece = wout.at[k, partner, columns(0, half)]
-            pltpu.make_async_copy(piece, piece, oc_recv.at[2 * k + half]).wait()
+    def arrived(index, part, sem):
+        pltpu.make_async_copy(place(index, part), place(index, part), sem.at[index]).wait()
+
+    def summed(k):
+        pltpu.make_async_copy(wout.at[k, partner], wout.at[k, partner], oc_recv.at[k]).wait()
         for h in range(2):
 
             @pl.when((z != k) | (c != h))
@@ -397,17 +399,43 @@
         term = jnp.dot(lhs[...], wout[k], preferred_element_type=F32)
         sums[...] = term if k == 0 else sums[...] + term
 
+    for k in range(nz):
+        arrived(k, kind, s1_recv)
+
+        @pl.when(z != k)
+        def _():
+            forwarded(k, kind, 0).start()
+            forwarded(k, kind, 1).start()
+
+        handed(k, kind).start()
+    for k in range(nz):
+        arrived(k, share(-1), left_in)
+        arrived(k, share(1), right_in)
+
+        @pl.when(z != k)
+        def _():
+            relayed(k).start()
+
+        handed(k, share(-1)).start()
+        handed(k, share(1)).start()
+    for k in range(nz):
+        arrived(k, share(2), far_in)
+        handed(k, share(2)).start()
+        if k >= 2:
+            summed(k - 2)
+    summed(nz - 2)
+    summed(nz - 1)
+
     def scatter(slot, there, target):
         return pltpu.make_async_remote_copy(
             src_ref=c_send.at[slot, target],
             dst_ref=c_recv.at[c * nx + x],
-            send_sem=cs_sem.at[2 * slot + target],
-            recv_sem=cr_sem.at[c * nx + x],
+            send_sem=cs_sem,
+            recv_sem=cr_sem,
             device_id=(y, z, there, target),
             device_id_type=MESH,
         )
 
-    c_copies = []
     for i, d in enumerate([*distances(nx), 0]):
         there = lax.rem(x + d, nx)
         block = sums[:, pl.ds(pl.multiple_of(there * 128, 128), 128)]
@@ -415,13 +443,9 @@
         c_send[i, 0] = jnp.where(side, top, pltpu.roll(bottom, CH, 1)).astype(BF16)
         c_send[i, 1] = jnp.where(side, pltpu.roll(top, CH, 1), bottom).astype(BF16)
         for target in (c, other) if d else (other,):
-            copy = scatter(i, there, target)
-            copy.start()
-            c_copies.append(copy)
+            scatter(i, there, target).start()
     c_recv[c * nx + x] = c_send[nx - 1, c]
-    for d in range(1, 2 * nx):
-        sender = lax.rem(c * nx + x + d, 2 * nx)
-        pltpu.make_async_copy(c_recv.at[0], c_recv.at[0], cr_sem.at[sender]).wait()
+    waited(c_recv.at[pl.ds(0, 2 * nx - 1)], cr_sem)
     pieces = []
     for h in range(2):
         added = c_recv[h * nx].astype(F32)
@@ -431,18 +455,14 @@
     result = jnp.concatenate(pieces, axis=0)
     out[...] = result.T[0:CH, :].astype(BF16)
 
-    for copy in (*e_copies, *c_copies, halo_copy, gather(z, other)):
+    for copy in (*e_copies, halo_copy):
         copy.wait_send()
-    for k in range(nz):
-        handed(k, 0).wait_send()
-        handed(k, 1).wait_send()
-
-        @pl.when(z != k)
-        def _():
-            spread(k).wait_send()
-            forwarded(k).wait_send()
-            gather(k, c).wait_send()
-            gather(k, other).wait_send()
+    rows = pl.ds(0, nz - 1)
+    waited(wout.at[rows, mine, pl.ds(0, width)], s1_send)
+    waited(wout.at[rows, mine, pl.ds(0, 3 * width)], s2_send)
+    waited(wout.at[:, mine], oc_send)
+    waited(a_recv.at[pl.ds(0, 2 * nz - 1)], as_sem)
+    waited(c_recv.at[pl.ds(0, 2 * nx - 1)], cs_sem)
 
 
 def local(
@@ -491,19 +511,19 @@
             pltpu.VMEM((2 * nx, QUARTER, 128), BF16),
             dma((WIDTH // TOKEN_CHUNK,)),
             dma((WIDTH // WEIGHT_CHUNK,)),
+            dma,
             dma((nz,)),
+            dma,
+            dma((3, nz)),
+            dma,
             dma((nz,)),
-            dma((nz,)),
-            dma((nz,)),
-            dma((2 * nz,)),
-            dma((2 * nz,)),
             dma((2,)),
             dma((3,)),
             dma((3,)),
+            dma,
             dma((2 * nz,)),
-            dma((2 * nz,)),
-            dma((2 * nx,)),
-            dma((2 * nx,)),
+            dma,
+            dma,
             pltpu.SemaphoreType.REGULAR((2 * nz,)),
         ],
         compiler_params=pltpu.CompilerParams(

time: 48.5 us -> 47.6 us (0.981)
  Pallas kernels: 46.9 us -> 46 us
    pallas_call x1, Pallas kernels: 46.9 us -> 46 us  [local(): pl.pallas_call(functools.partial(kernel, sizes), out_shape=jax.ShapeDtype...]
where the time goes in v3:
time: 47.6 us; the launch traced here: 47.4 us
  Pallas kernels  46 us (97%)
  local copies, waits for them, and re-layouts  1.38 us (3%)
    pallas_call x1, Pallas kernels, local(): pl.pallas_call(functools.partial(kernel, sizes), out_shape=jax.ShapeDtype...  46 us
    unnamed x1, local copies, waits for them, and re-layouts  1.38 us

profile of v3, /device:TPU:1, one launch (start us, length us, event | category | flops | bytes accessed | tf_op | source)
XLA Modules:
  0.0 47.4 jit_solution(13871545636822952)
XLA Ops:
  0.0 46.0 %shard_map.91 = bf16[64,192]{1,0:T(8,128)(2,1)} custom-call(bf16[192,8192]{1,0:T(8,128)(2,1)} %tokens.1, f32[1,8192]{1,0:T(1,128)} %bitcast.9, bf16[192,8192]{1,0:T(8,128)(2,1)} %bitcast.7, f32[3,3,64]{2,1,0:T(4,128)} %taps_in.1, f32[16,64]{1,0:T(8,128)} %rates_in.1, f32[16,64]{1,0:T(8,128)} %residues_in.1, f32[1,64]{1,0:T(1,128)} %bitcast.11, ...), custom_call_target="tpu_custom_call" | custom-call | tf_op jit(solution)/shard_map/pallas_call | solution.py:477
  46.0 1.4 %copy.11 = bf16[192,64]{0,1:T(8,128)(2,1)} copy(bf16[192,64]{0,1:T(8,128)(2,1)} %bitcast.8) | data formatting | bytes 49152

commit v4 on v3

--- a/solution.py
+++ b/solution.py
@@ -41,7 +41,7 @@
     out,
     gain, taps, rates, residues, skip, ids, small_sem,
     tok, win, wout, proj, halo, growth, weighted, visible, product, query, acc,
-    lag_one, lag_two, survives, ends, incoming, a_send, a_recv, lhs, sums, c_send, c_recv,
+    lag_one, lag_two, survives, ends, incoming, carry, a_send, a_recv, lhs, sums, c_send, c_recv,
     tok_sem, win_sem, s1_send, s1_recv, s2_send, s2_recv, oc_send, oc_recv,
     halo_sem, e_send, e_recv, as_sem, ar_sem, cs_sem, cr_sem, z_ready,
 ):
@@ -221,15 +221,19 @@
     proj[8 : 8 + ROWS, 0:128] = rounded[:, 0:128]
     value_part = rounded[:, 128 : 3 * CH]
     proj[8 : 8 + ROWS, 128:256] = jnp.concatenate([value_part, value_part], axis=1)
-    halo_copy = pltpu.make_async_remote_copy(
-        src_ref=proj.at[pl.ds(ROWS, 8)],
-        dst_ref=halo,
-        send_sem=halo_sem.at[0],
-        recv_sem=halo_sem.at[1],
-        device_id=at_y(1),
-        device_id_type=MESH,
-    )
-    halo_copy.start()
+    def send_halo():
+        return pltpu.make_async_remote_copy(
+            src_ref=proj.at[pl.ds(ROWS, 8)],
+            dst_ref=halo,
+            send_sem=halo_sem.at[0],
+            recv_sem=halo_sem.at[1],
+            device_id=at_y(1),
+            device_id_type=MESH,
+        )
+
+    @pl.when(y + 1 < ny)
+    def _():
+        send_halo().start()
 
     for d in range(1, EARLY + 1):
         spread_later(d)
@@ -277,8 +281,11 @@
         total = total + growth[:, lanes] * inside
     last = jnp.concatenate(last, axis=0)
 
-    halo_copy.wait_recv()
-    proj[0:8, :] = halo[...] * reach[1]
+    @pl.when(y >= 1)
+    def _():
+        waited(halo, halo_sem.at[1])
+        proj[0:8, :] = halo[...]
+
     query_top, product_top = filtered(8)
     change = product_top - product[0:8, :]
     query[0:8, :] = query_top
@@ -288,28 +295,34 @@
     ends[...] = jnp.exp((CENTER + 1.0 - ROWS) * rate) * (
         last + whole * (change_zero + change_one)
     )
-    e_copies = []
-    for k in range(3):
-        copy = pltpu.make_async_remote_copy(
+    def send_ends(k):
+        return pltpu.make_async_remote_copy(
             src_ref=ends,
-            dst_ref=incoming.at[k],
-            send_sem=e_send.at[k],
-            recv_sem=e_recv.at[k],
-            device_id=at_y(k + 1),
-            device_id_type=MESH,
-        )
-        copy.start()
-        e_copies.append(copy)
+            dst_ref=incoming.at[k - 1],
+            send_sem=e_send.at[k - 1],
+            recv_sem=e_recv.at[k - 1],
+            device_id=at_y(k),
+            device_id_type=MESH,
+        )
+
+    for k in range(1, REACH + 1):
+
+        @pl.when(y + k < ny)
+        def _():
+            send_ends(k).start()
 
     spread_later(EARLY + 1)
 
-    for k in range(3):
-        e_copies[k].wait_recv()
-    carried = reach[1] * incoming[0]
-    for k in (1, 2):
-        reached = jnp.where(before[0] == before[k], reach[k + 1], 0.0)
-        carried = carried + reached * jnp.exp(-float(ROWS * k) * rate) * incoming[k]
-    carried = jnp.exp(-(CENTER + 1.0) * rate) * carried + change_zero
+    carry[...] = jnp.zeros((PAIRS, 128), F32)
+    for k in range(1, REACH + 1):
+
+        @pl.when(y >= k)
+        def _():
+            waited(incoming.at[k - 1], e_recv.at[k - 1])
+            reached = jnp.where(before[0] == before[k - 1], 1.0, 0.0)
+            carry[...] += reached * jnp.exp(-float(ROWS * (k - 1)) * rate) * incoming[k - 1]
+
+    carried = jnp.exp(-(CENTER + 1.0) * rate) * carry[...] + change_zero
     entering = jnp.zeros((ROWS, 128), F32)
     changed = jnp.zeros((ROWS, 128), F32)
     for g in range(PAIRS):
@@ -455,8 +468,16 @@
     result = jnp.concatenate(pieces, axis=0)
     out[...] = result.T[0:CH, :].astype(BF16)
 
-    for copy in (*e_copies, halo_copy):
-        copy.wait_send()
+    @pl.when(y + 1 < ny)
+    def _():
+        send_halo().wait_send()
+
+    for k in range(1, REACH + 1):
+
+        @pl.when(y + k < ny)
+        def _():
+            send_ends(k).wait_send()
+
     rows = pl.ds(0, nz - 1)
     waited(wout.at[rows, mine, pl.ds(0, width)], s1_send)
     waited(wout.at[rows, mine, pl.ds(0, 3 * width)], s2_send)
@@ -502,7 +523,8 @@
             pltpu.VMEM((ROWS, 128), F32),
             pltpu.VMEM((ROWS, 128), F32),
             pltpu.VMEM((PAIRS, 128), F32),
-            pltpu.VMEM((3, PAIRS, 128), F32),
+            pltpu.VMEM((REACH, PAIRS, 128), F32),
+            pltpu.VMEM((PAIRS, 128), F32),
             pltpu.VMEM((2, QUARTER, 128), BF16),
             pltpu.VMEM((2 * nz, QUARTER, 128), BF16),
             pltpu.VMEM((HALF, 2 * CH), BF16),

time: 47.6 us -> 46.9 us (0.985)
  Pallas kernels: 46 us -> 45.4 us
    pallas_call x1, Pallas kernels: 46 us -> 45.4 us  [local(): pl.pallas_call(functools.partial(kernel, sizes), out_shape=jax.ShapeDtype...]
where the time goes in v4:
time: 46.9 us; the launch traced here: 46.7 us
  Pallas kernels  45.4 us (97%)
  local copies, waits for them, and re-layouts  1.38 us (3%)
    pallas_call x1, Pallas kernels, local(): pl.pallas_call(functools.partial(kernel, sizes), out_shape=jax.ShapeDtype...  45.4 us
    unnamed x1, local copies, waits for them, and re-layouts  1.38 us

profile of v4, /device:TPU:1, one launch (start us, length us, event | category | flops | bytes accessed | tf_op | source)
XLA Modules:
  0.0 46.7 jit_solution(16603833379462774466)
XLA Ops:
  0.0 45.4 %shard_map.91 = bf16[64,192]{1,0:T(8,128)(2,1)} custom-call(bf16[192,8192]{1,0:T(8,128)(2,1)} %tokens.1, f32[1,8192]{1,0:T(1,128)} %bitcast.9, bf16[192,8192]{1,0:T(8,128)(2,1)} %bitcast.7, f32[3,3,64]{2,1,0:T(4,128)} %taps_in.1, f32[16,64]{1,0:T(8,128)} %rates_in.1, f32[16,64]{1,0:T(8,128)} %residues_in.1, f32[1,64]{1,0:T(1,128)} %bitcast.11, ...), custom_call_target="tpu_custom_call" | custom-call | tf_op jit(solution)/shard_map/pallas_call | solution.py:498
  45.4 1.4 %copy.11 = bf16[192,64]{0,1:T(8,128)(2,1)} copy(bf16[192,64]{0,1:T(8,128)(2,1)} %bitcast.8) | data formatting | bytes 49152
